TPU v7x, 256 devices: a whole 4x4x8 slice. The times are simulated.
256 devices in a mesh: slab: 64 (over y, x_lo, z), grp: 4 (over x_hi, core).
Axes of the slice: x: 4 (x_hi: 2, x_lo: 2; x = x_hi * 2 + x_lo), y: 4, z: 8, core: 2. Of those that a mesh axis runs over, the one named last changes fastest.
Arguments:
- tiles: bfloat16 [768, 27, 36864], P(('slab', 'grp')), may hold values from -0.0390625 to 0.0390625
- neighbours: int32 [768, 27], P('slab'), may hold values from 0 to 767, as said below
- t_cur: bfloat16 [768, 192, 512], P('slab', None, 'grp'), may hold values from -6 to 6
- t_prev: float32 [768, 192, 512], P('slab', None, 'grp'), may hold values from -6 to 6
- probes: float32 [768, 192, 512], P('slab', None, 'grp'), may hold values from -18 to 18
Outputs:
- t_next: float32 [768, 192, 512], P('slab', None, 'grp')
- moments: float32 [2, 512], P(None, 'grp')
Inputs may be any that keep to these rules, and one draw needn't show every extreme that they name: Block b lies in slab b // 12; each of its neighbours lies in the same slab or in one of the two slabs beside it, the last slab being beside the first.
All inputs are finite; a program needn't handle non-finite values.
Results may differ from a plain program's by a relative error of at most 0.0003.
Values may be sent and summed in bfloat16 or wider, within the bound.
A program may use at most 192 MiB of HBM per device.

v0:
```python
import math
import jax
import jax.numpy as jnp
from jax import lax
from jax.sharding import PartitionSpec as P


def with_halo(value, sides, width):
    for axis, dim in sides:
        size, length = (lax.axis_size(axis), value.shape[dim])
        up = [(i, (i + 1) % size) for i in range(size)]
        down = [(j, i) for i, j in up]
        last = lax.slice_in_dim(value, length - width, length, axis=dim)
        leading = lax.slice_in_dim(value, 0, width, axis=dim)
        before = lax.ppermute(last, axis, up)
        after = lax.ppermute(leading, axis, down)
        value = jnp.concatenate([before, value, after], axis=dim)
    return value


def apply_rows(tile_rows, padded, locals_rows):
    width = padded.shape[1]
    squares = tile_rows.reshape(tile_rows.shape[:2] + (width, width))
    near = jnp.take(padded, locals_rows.reshape(-1), axis=0)
    near = near.reshape(locals_rows.shape + padded.shape[1:])
    return jnp.einsum("bkrc,bkcp->brp", squares, near, preferred_element_type=jnp.float32)


def shards(tiles, neighbours, t_cur, t_prev, probes):
    blocks_slab = t_cur.shape[0]
    slab_count = lax.axis_size("slab")
    my_slab = lax.axis_index("slab")
    slab_near = neighbours // blocks_slab
    local_ids = (slab_near - my_slab + 1) % slab_count * blocks_slab + neighbours % blocks_slab
    rows_dev = tiles.shape[0]
    mine = lax.dynamic_slice_in_dim(local_ids, lax.axis_index("grp") * rows_dev, rows_dev, 0)
    whole = lax.all_gather(t_cur, "grp", axis=2, tiled=True)
    padded = with_halo(whole, (("slab", 0),), blocks_slab)
    rows_image = apply_rows(tiles, padded, mine)
    image = lax.all_to_all(rows_image, "grp", split_axis=2, concat_axis=0, tiled=True)
    t_next = 2.0 * image - t_prev
    first = jnp.sum(probes * t_next, axis=(0, 1))
    second = jnp.sum(t_cur.astype(jnp.float32) * t_next, axis=(0, 1))
    first, second = lax.psum((first, second), "slab")
    factor = 1.0 / math.sqrt(slab_count * blocks_slab * t_cur.shape[1])
    moments = jnp.stack([first, second]) * factor
    return (t_next, moments)


def solution(mesh):
    placed = (
        P(("slab", "grp"), None, None),
        P("slab", None),
        P("slab", None, "grp"),
        P("slab", None, "grp"),
        P("slab", None, "grp"),
    )
    return jax.shard_map(
        shards,
        mesh=mesh,
        in_specs=placed,
        out_specs=(P("slab", None, "grp"), P(None, "grp")),
        check_vma=False,
    )
```

profile of v0, /device:TPU:0, one launch (start us, length us, event | category | flops | bytes accessed | tf_op | source)
XLA Modules:
  0.0 328.1 jit_solution(8495705729886352172)
XLA Ops:
  7.2 0.0 all-gather.2.cloned.1.call-start
  7.2 0.7 all-gather.2.cloned.1.call-update
  7.9 34.1 %all-gather.2.cloned.1.call-done = bf16[12,192,512]{2,1,0:T(8,128)(2,1)} async-done(((bf16[12,192,128]{2,1,0:T(8,128)(2,1)}), bf16[12,192,512]{2,1,0:T(8,128)(2,1)}) %all-gather.2.cloned.1.call-update) | async-done | bytes 2359312 | tf_op jit(solution)/shard_map/all_gather | solution.py:37
  42.0 1.6 collective-permute-start
  43.6 4.7 %collective-permute-start.1 = (bf16[12,192,512]{2,1,0:T(8,128)(2,1)}, bf16[12,192,512]{2,1,0:T(8,128)(2,1)}, u32[]{:S(2)}, u32[]{:S(2)}) collective-permute-start(bf16[12,192,512]{2,1,0:T(8,128)(2,1)} %all-gather.2.cloned.1.call-done), channel_id=1, source_target_pairs={{4,0},{8,4},{12,8},{16,12},{20,16},{24,20},{28,24},{32,28},{36,32}... | collective-permute-start | bytes 7077896 | tf_op jit(solution)/shard_map/ppermute | solution.py:16
  48.3 0.7 broadcast_compare_fusion
  49.0 0.7 fusion.16
  49.7 0.1 reshape.51
  49.8 0.0 copy-start
  49.8 12.2 %reshape.52 = bf16[3,27,192,192]{3,2,1,0:T(8,128)(2,1)} reshape(bf16[3,27,36864]{2,1,0:T(8,128)(2,1)} %param.5) | data formatting | bytes 11943936 | tf_op jit(solution)/shard_map/reshape | solution.py:23
  62.0 37.9 %collective-permute-done = bf16[12,192,512]{2,1,0:T(8,128)(2,1)} collective-permute-done((bf16[12,192,512]{2,1,0:T(8,128)(2,1)}, bf16[12,192,512]{2,1,0:T(8,128)(2,1)}, u32[]{:S(2)}, u32[]{:S(2)}) %collective-permute-start) | collective-permute-done | bytes 2359328 | tf_op jit(solution)/shard_map/ppermute | solution.py:15
  100.0 0.0 collective-permute-done.1
  100.0 0.0 copy-done
  100.0 5.9 %pad_maximum_fusion = bf16[36,192,512]{2,1,0:T(8,128)(2,1)} fusion(bf16[12,192,512]{2,1,0:T(8,128)(2,1)} %collective-permute-done.1, bf16[12,192,512]{2,1,0:T(8,128)(2,1)S(1)} %copy-done, bf16[12,192,512]{2,1,0:T(8,128)(2,1)} %collective-permute-done), kind=kLoop, calls=%fused_computation.5 | loop fusion | flops 7077888 | bytes 14155776 | tf_op jit(solution)/shard_map/concatenate | solution.py:17
  105.8 11.3 %gather_fusion = bf16[81,192,512]{2,1,0:T(8,128)(2,1)} fusion(bf16[36,192,512]{2,1,0:T(8,128)(2,1)} %pad_maximum_fusion, s32[1024]{0:T(1024)S(1)} %pad_clamp_fusion), kind=kCustom, calls=%fused_computation | custom fusion | bytes 31850820 | tf_op jit(solution)/shard_map/jit(_take)/gather | solution.py:24
  117.2 10.4 %fusion.4 = f32[3,192,512]{2,1,0:T(8,128)S(1)} fusion(bf16[3,27,192,192]{3,2,1,0:T(8,128)(2,1)} %reshape.52, bf16[3,27,192,512]{3,2,1,0:T(8,128)(2,1)} %bitcast.17, pred[3,27]{1,0:T(4,128)(4,1)S(1)} %get-tuple-element.7), kind=kOutput, calls=%fused_computation.6 | convolution fusion | flops 3065610240 | bytes 23076944 | tf_op jit(solution)/shard_map/bkrc,bkcp->brp/dot_general | solution.py:26
  127.6 0.9 copy.8
  128.5 29.9 %all_to_all.4 = f32[3,192,512]{1,0,2:T(4,128)S(1)} all-to-all(f32[3,192,512]{1,0,2:T(4,128)S(1)} %copy.8), channel_id=1, replica_groups=mesh['slab'=64,'grp'=4] {'grp'}, dimensions={2} | all-to-all | bytes 2359296 | tf_op jit(solution)/shard_map/all_to_all | solution.py:40
  158.4 0.5 broadcast_multiply_fusion
  158.8 0.7 copy.9
  159.5 3.1 multiply_reduce_fusion.1
  162.6 158.1 %all-reduce = (f32[1,128]{1,0:T(1,128)S(1)}, f32[1,128]{1,0:T(1,128)S(1)}) all-reduce(f32[1,128]{1,0:T(1,128)S(1)} %bitcast.20, f32[1,128]{1,0:T(1,128)S(1)} %bitcast.19), channel_id=1, replica_groups=mesh['slab'=64,'grp'=4] {'slab'}, use_global_device_ids=true, to_apply=%region_3.4 | all-reduce | flops 256 | bytes 2048 | tf_op jit(solution)/shard_map/psum | solution.py:44
  320.7 0.6 maximum_multiply_fusion
  (3 shorter events, 0.0 us)
Async XLA Ops:
  7.2 34.8 %all-gather.2.cloned.1.call-start = ((), (), s32[]{:S(2)}) async-start(), calls=%async_computation.1 | async-start | bytes 2949120 | tf_op jit(solution)/shard_map/all_gather | solution.py:37
  42.0 57.9 %collective-permute-start = (bf16[12,192,512]{2,1,0:T(8,128)(2,1)}, bf16[12,192,512]{2,1,0:T(8,128)(2,1)}, u32[]{:S(2)}, u32[]{:S(2)}) collective-permute-start(bf16[12,192,512]{2,1,0:T(8,128)(2,1)} %all-gather.2.cloned.1.call-done), channel_id=1, source_target_pairs={{0,4},{4,8},{8,12},{12,16},{16,20},{20,24},{24,28},{28,32},{32,36}... | collective-permute-start | bytes 7077896 | tf_op jit(solution)/shard_map/ppermute | solution.py:15
  43.6 56.4 %collective-permute-start.1 = (bf16[12,192,512]{2,1,0:T(8,128)(2,1)}, bf16[12,192,512]{2,1,0:T(8,128)(2,1)}, u32[]{:S(2)}, u32[]{:S(2)}) collective-permute-start(bf16[12,192,512]{2,1,0:T(8,128)(2,1)} %all-gather.2.cloned.1.call-done), channel_id=1, source_target_pairs={{4,0},{8,4},{12,8},{16,12},{20,16},{24,20},{28,24},{32,28},{36,32}... | collective-permute-start | bytes 7077896 | tf_op jit(solution)/shard_map/ppermute | solution.py:16
  49.8 50.2 %copy-start = (bf16[12,192,512]{2,1,0:T(8,128)(2,1)S(1)}, bf16[12,192,512]{2,1,0:T(8,128)(2,1)}, u32[]{:S(2)}) copy-start(bf16[12,192,512]{2,1,0:T(8,128)(2,1)} %all-gather.2.cloned.1.call-done) | copy-start | bytes 7077892
Sparse Core Ops, SparseCore 0:
  9.8 32.1 all-gather.1
where the time goes:
time: 329 us; the launch traced here: 328 us
  blocking collectives  188 us (57%)
  waiting for transfers between devices  72.7 us (22%)
  local copies, waits for them, and re-layouts  25.3 us (8%)
  between operations  14.1 us (4%)
  other arithmetic  11.5 us (3%)
  matrix products  10.4 us (3%)
  starting transfers between devices  6.28 us (2%)
    psum x1, blocking collectives, shards(): first, second = lax.psum((first, second), 'slab')  158 us
    ppermute x1, waiting for transfers between devices, with_halo(): before = lax.ppermute(last, axis, up)  37.9 us
    all_gather x1, waiting for transfers between devices, shards(): whole = lax.all_gather(t_cur, 'grp', axis=2, tiled=True)  34.1 us
    all_to_all x1, blocking collectives, shards(): lax.all_to_all(rows_image, 'grp', split_axis=2, concat_axis=0, tiled=True)  29.9 us
    reshape x1, local copies, waits for them, and re-layouts, apply_rows(): squares = tile_rows.reshape(tile_rows.shape[:2] + (width, width))  12.2 us
    gather x1, local copies, waits for them, and re-layouts, apply_rows(): near = jnp.take(padded, locals_rows.reshape(-1), axis=0)  11.3 us
    dot_general x1, matrix products, apply_rows(): jnp.einsum('bkrc,bkcp->brp', squares, near, preferred_element_type=jnp.fl...  10.4 us
  transfers between devices with their start and end apart: 3, of which 2 were waited for; matrix products, arithmetic and copies ran while one was open for 4% of the time, Pallas kernels for 0%

commit v1 on v0

--- a/solution.py
+++ b/solution.py
@@ -34,7 +34,9 @@
     local_ids = (slab_near - my_slab + 1) % slab_count * blocks_slab + neighbours % blocks_slab
     rows_dev = tiles.shape[0]
     mine = lax.dynamic_slice_in_dim(local_ids, lax.axis_index("grp") * rows_dev, rows_dev, 0)
-    whole = lax.all_gather(t_cur, "grp", axis=2, tiled=True)
+    whole = jnp.concatenate(
+        lax.all_to_all(jnp.stack([t_cur] * lax.axis_size("grp")), "grp", 0, 0), axis=2
+    )
     padded = with_halo(whole, (("slab", 0),), blocks_slab)
     rows_image = apply_rows(tiles, padded, mine)
     image = lax.all_to_all(rows_image, "grp", split_axis=2, concat_axis=0, tiled=True)

time: 329 us -> 316 us (0.960)
  waiting for transfers between devices: 72.7 us -> 38.7 us
  blocking collectives: 188 us -> 221 us
  between operations: 14.1 us -> 0.69 us
    all_gather x1 -> x0, waiting for transfers between devices: 34.1 us -> none  [shards(): whole = lax.all_gather(t_cur, 'grp', axis=2, tiled=True)]
    all_to_all x0 -> x1, blocking collectives: none -> 32.5 us  [shards(): lax.all_to_all(jnp.stack([t_cur] * lax.axis_size('grp')), 'grp', 0, 0)]
  transfers between devices with their start and end apart: 3 -> 2, of which waited for: 2 -> 1; matrix products, arithmetic and copies ran while one was open for 4% -> 4% of each run, Pallas kernels for 0% -> 0%
where the time goes in v1:
time: 316 us
  blocking collectives  221 us (70%)
  waiting for transfers between devices  38.7 us (12%)
  local copies, waits for them, and re-layouts  27.1 us (9%)
  matrix products  10.4 us (3%)
  other arithmetic  10 us (3%)
  starting transfers between devices  8.38 us (3%)
    psum x1, blocking collectives, shards(): first, second = lax.psum((first, second), 'slab')  158 us
    ppermute x1, waiting for transfers between devices, with_halo(): before = lax.ppermute(last, axis, up)  38.6 us
    all_to_all x1, blocking collectives, shards(): lax.all_to_all(jnp.stack([t_cur] * lax.axis_size('grp')), 'grp', 0, 0)  32.5 us
    all_to_all x1, blocking collectives, shards(): lax.all_to_all(rows_image, 'grp', split_axis=2, concat_axis=0, tiled=True)  29.7 us
    reshape x1, local copies, waits for them, and re-layouts, apply_rows(): squares = tile_rows.reshape(tile_rows.shape[:2] + (width, width))  12.1 us
    gather x1, local copies, waits for them, and re-layouts, apply_rows(): near = jnp.take(padded, locals_rows.reshape(-1), axis=0)  11.3 us
    dot_general x1, matrix products, apply_rows(): jnp.einsum('bkrc,bkcp->brp', squares, near, preferred_element_type=jnp.fl...  10.4 us
    ppermute x1, starting transfers between devices, with_halo(): after = lax.ppermute(leading, axis, down)  6.51 us
  transfers between devices with their start and end apart: 2, of which 1 were waited for; matrix products, arithmetic and copies ran while one was open for 4% of the time, Pallas kernels for 0%

profile of v1, /device:TPU:0, one launch (start us, length us, event | category | flops | bytes accessed | tf_op | source)
XLA Modules:
  0.0 315.7 jit_solution(9845473239247121375)
XLA Ops:
  0.6 1.6 stack.16
  2.3 32.5 %all_to_all.14 = bf16[4,12,192,128]{3,2,1,0:T(8,128)(2,1)S(1)} all-to-all(bf16[4,12,192,128]{3,2,1,0:T(8,128)(2,1)S(1)} %stack.16), channel_id=1, replica_groups=mesh['slab'=64,'grp'=4] {'grp'}, dimensions={0} | all-to-all | bytes 4718592 | tf_op jit(solution)/shard_map/all_to_all | solution.py:38
  34.7 0.0 copy-start
  34.7 0.3 copy_bitcast_fusion
  35.1 1.9 collective-permute-start
  36.9 6.5 %collective-permute-start.1 = (bf16[12,192,512]{2,1,0:T(8,128)(2,1)S(1)}, bf16[12,192,512]{2,1,0:T(8,128)(2,1)}, u32[]{:S(2)}, u32[]{:S(2)}) collective-permute-start(bf16[12,192,512]{2,1,0:T(8,128)(2,1)S(1)} %copy_bitcast_fusion), channel_id=1, source_target_pairs={{4,0},{8,4},{12,8},{16,12},{20,16},{24,20},{28,24},{32,28},{36,32}... | collective-permute-start | bytes 7077896 | tf_op jit(solution)/shard_map/ppermute | solution.py:16
  43.4 0.0 copy-done
  43.5 0.1 reshape.61
  43.6 12.1 %reshape.62 = bf16[3,27,192,192]{3,2,1,0:T(8,128)(2,1)} reshape(bf16[3,27,36864]{2,1,0:T(8,128)(2,1)} %param.5) | data formatting | bytes 11943936 | tf_op jit(solution)/shard_map/reshape | solution.py:23
  55.7 38.6 %collective-permute-done = bf16[12,192,512]{2,1,0:T(8,128)(2,1)} collective-permute-done((bf16[12,192,512]{2,1,0:T(8,128)(2,1)S(1)}, bf16[12,192,512]{2,1,0:T(8,128)(2,1)}, u32[]{:S(2)}, u32[]{:S(2)}) %collective-permute-start) | collective-permute-done | bytes 2359328 | tf_op jit(solution)/shard_map/ppermute | solution.py:15
  94.3 0.0 collective-permute-done.1
  94.3 5.8 %pad_maximum_fusion = bf16[36,192,512]{2,1,0:T(8,128)(2,1)} fusion(bf16[12,192,512]{2,1,0:T(8,128)(2,1)} %collective-permute-done.1, bf16[12,192,512]{2,1,0:T(8,128)(2,1)S(1)} %copy_bitcast_fusion, bf16[12,192,512]{2,1,0:T(8,128)(2,1)} %collective-permute-done), kind=kLoop, calls=%fused_computation.5 | loop fusion | flops 7077888 | bytes 14155776 | tf_op jit(solution)/shard_map/concatenate | solution.py:17
  100.2 11.3 %gather_fusion = bf16[81,192,512]{2,1,0:T(8,128)(2,1)} fusion(bf16[36,192,512]{2,1,0:T(8,128)(2,1)} %pad_maximum_fusion, s32[1024]{0:T(1024)S(1)} %pad_clamp_fusion), kind=kCustom, calls=%fused_computation | custom fusion | bytes 31850820 | tf_op jit(solution)/shard_map/jit(_take)/gather | solution.py:24
  111.5 10.4 %fusion.4 = f32[3,192,512]{2,1,0:T(8,128)S(1)} fusion(bf16[3,27,192,192]{3,2,1,0:T(8,128)(2,1)} %reshape.62, bf16[3,27,192,512]{3,2,1,0:T(8,128)(2,1)} %bitcast.23, pred[3,27]{1,0:T(4,128)(4,1)S(1)} %get-tuple-element.7), kind=kOutput, calls=%fused_computation.7 | convolution fusion | flops 3065610240 | bytes 23076944 | tf_op jit(solution)/shard_map/bkrc,bkcp->brp/dot_general | solution.py:26
  121.9 0.9 copy.10
  122.9 29.7 %all_to_all.15 = f32[3,192,512]{1,0,2:T(4,128)S(1)} all-to-all(f32[3,192,512]{1,0,2:T(4,128)S(1)} %copy.10), channel_id=1, replica_groups=mesh['slab'=64,'grp'=4] {'grp'}, dimensions={2} | all-to-all | bytes 2359296 | tf_op jit(solution)/shard_map/all_to_all | solution.py:42
  152.6 0.5 broadcast_multiply_fusion
  153.0 0.7 copy.11
  153.7 3.1 multiply_reduce_fusion.1
  156.8 158.3 %all-reduce = (f32[1,128]{1,0:T(1,128)S(1)}, f32[1,128]{1,0:T(1,128)S(1)}) all-reduce(f32[1,128]{1,0:T(1,128)S(1)} %bitcast.26, f32[1,128]{1,0:T(1,128)S(1)} %bitcast.25), channel_id=1, replica_groups=mesh['slab'=64,'grp'=4] {'slab'}, use_global_device_ids=true, to_apply=%region_3.4 | all-reduce | flops 256 | bytes 2048 | tf_op jit(solution)/shard_map/psum | solution.py:46
  315.2 0.6 maximum_multiply_fusion
  (5 shorter events, 0.1 us)
Async XLA Ops:
  34.7 8.7 %copy-start = (s32[12,27]{1,0:T(8,128)S(1)}, s32[12,27]{1,0:T(8,128)}, u32[]{:S(2)}) copy-start(s32[12,27]{1,0:T(8,128)} %param.6) | copy-start | bytes 3892
  35.1 59.3 %collective-permute-start = (bf16[12,192,512]{2,1,0:T(8,128)(2,1)S(1)}, bf16[12,192,512]{2,1,0:T(8,128)(2,1)}, u32[]{:S(2)}, u32[]{:S(2)}) collective-permute-start(bf16[12,192,512]{2,1,0:T(8,128)(2,1)S(1)} %copy_bitcast_fusion), channel_id=1, source_target_pairs={{0,4},{4,8},{8,12},{12,16},{16,20},{20,24},{24,28},{28,32},{32,36}... | collective-permute-start | bytes 7077896 | tf_op jit(solution)/shard_map/ppermute | solution.py:15
  36.9 57.4 %collective-permute-start.1 = (bf16[12,192,512]{2,1,0:T(8,128)(2,1)S(1)}, bf16[12,192,512]{2,1,0:T(8,128)(2,1)}, u32[]{:S(2)}, u32[]{:S(2)}) collective-permute-start(bf16[12,192,512]{2,1,0:T(8,128)(2,1)S(1)} %copy_bitcast_fusion), channel_id=1, source_target_pairs={{4,0},{8,4},{12,8},{16,12},{20,16},{24,20},{28,24},{32,28},{36,32}... | collective-permute-start | bytes 7077896 | tf_op jit(solution)/shard_map/ppermute | solution.py:16

commit v2 on v0

--- a/solution.py
+++ b/solution.py
@@ -37,7 +37,10 @@
     whole = lax.all_gather(t_cur, "grp", axis=2, tiled=True)
     padded = with_halo(whole, (("slab", 0),), blocks_slab)
     rows_image = apply_rows(tiles, padded, mine)
-    image = lax.all_to_all(rows_image, "grp", split_axis=2, concat_axis=0, tiled=True)
+    image = jnp.concatenate(
+        lax.all_to_all(jnp.stack(jnp.split(rows_image, lax.axis_size("grp"), axis=2)), "grp", 0, 0),
+        axis=0,
+    )
     t_next = 2.0 * image - t_prev
     first = jnp.sum(probes * t_next, axis=(0, 1))
     second = jnp.sum(t_cur.astype(jnp.float32) * t_next, axis=(0, 1))

time: 329 us -> 315 us (0.957)
  blocking collectives: 188 us -> 178 us
    all_to_all x1, blocking collectives: 29.9 us -> 20.3 us  [shards(): lax.all_to_all(jnp.stack(jnp.split(rows_image, lax.axis_size('grp'), axis...]
where the time goes in v2:
time: 315 us
  blocking collectives  178 us (57%)
  waiting for transfers between devices  72.7 us (23%)
  local copies, waits for them, and re-layouts  23.8 us (8%)
  between operations  14.1 us (4%)
  matrix products  10.4 us (3%)
  other arithmetic  9.35 us (3%)
  starting transfers between devices  6.28 us (2%)
    psum x1, blocking collectives, shards(): first, second = lax.psum((first, second), 'slab')  158 us
    ppermute x1, waiting for transfers between devices, with_halo(): before = lax.ppermute(last, axis, up)  37.9 us
    all_gather x1, waiting for transfers between devices, shards(): whole = lax.all_gather(t_cur, 'grp', axis=2, tiled=True)  34.1 us
    all_to_all x1, blocking collectives, shards(): lax.all_to_all(jnp.stack(jnp.split(rows_image, lax.axis_size('grp'), axis...  20.3 us
    reshape x1, local copies, waits for them, and re-layouts, apply_rows(): squares = tile_rows.reshape(tile_rows.shape[:2] + (width, width))  12.2 us
    gather x1, local copies, waits for them, and re-layouts, apply_rows(): near = jnp.take(padded, locals_rows.reshape(-1), axis=0)  11.3 us
    dot_general x1, matrix products, apply_rows(): jnp.einsum('bkrc,bkcp->brp', squares, near, preferred_element_type=jnp.fl...  10.4 us
  transfers between devices with their start and end apart: 3, of which 2 were waited for; matrix products, arithmetic and copies ran while one was open for 4% of the time, Pallas kernels for 0%

profile of v2, /device:TPU:0, one launch (start us, length us, event | category | flops | bytes accessed | tf_op | source)
XLA Modules:
  0.0 315.0 jit_solution(16664144923861870334)
XLA Ops:
  7.2 0.0 all-gather.2.cloned.1.call-start
  7.2 0.7 all-gather.2.cloned.1.call-update
  7.9 34.1 %all-gather.2.cloned.1.call-done = bf16[12,192,512]{2,1,0:T(8,128)(2,1)} async-done(((bf16[12,192,128]{2,1,0:T(8,128)(2,1)}), bf16[12,192,512]{2,1,0:T(8,128)(2,1)}) %all-gather.2.cloned.1.call-update) | async-done | bytes 2359312 | tf_op jit(solution)/shard_map/all_gather | solution.py:37
  42.0 1.6 collective-permute-start
  43.6 4.7 %collective-permute-start.1 = (bf16[12,192,512]{2,1,0:T(8,128)(2,1)}, bf16[12,192,512]{2,1,0:T(8,128)(2,1)}, u32[]{:S(2)}, u32[]{:S(2)}) collective-permute-start(bf16[12,192,512]{2,1,0:T(8,128)(2,1)} %all-gather.2.cloned.1.call-done), channel_id=1, source_target_pairs={{4,0},{8,4},{12,8},{16,12},{20,16},{24,20},{28,24},{32,28},{36,32}... | collective-permute-start | bytes 7077896 | tf_op jit(solution)/shard_map/ppermute | solution.py:16
  48.3 0.7 broadcast_compare_fusion
  49.0 0.7 fusion.16
  49.7 0.1 reshape.50
  49.8 0.0 copy-start
  49.8 12.2 %reshape.51 = bf16[3,27,192,192]{3,2,1,0:T(8,128)(2,1)} reshape(bf16[3,27,36864]{2,1,0:T(8,128)(2,1)} %param.5) | data formatting | bytes 11943936 | tf_op jit(solution)/shard_map/reshape | solution.py:23
  62.0 37.9 %collective-permute-done = bf16[12,192,512]{2,1,0:T(8,128)(2,1)} collective-permute-done((bf16[12,192,512]{2,1,0:T(8,128)(2,1)}, bf16[12,192,512]{2,1,0:T(8,128)(2,1)}, u32[]{:S(2)}, u32[]{:S(2)}) %collective-permute-start) | collective-permute-done | bytes 2359328 | tf_op jit(solution)/shard_map/ppermute | solution.py:15
  100.0 0.0 collective-permute-done.1
  100.0 0.0 copy-done
  100.0 5.8 %pad_maximum_fusion = bf16[36,192,512]{2,1,0:T(8,128)(2,1)} fusion(bf16[12,192,512]{2,1,0:T(8,128)(2,1)} %collective-permute-done.1, bf16[12,192,512]{2,1,0:T(8,128)(2,1)S(1)} %copy-done, bf16[12,192,512]{2,1,0:T(8,128)(2,1)} %collective-permute-done), kind=kLoop, calls=%fused_computation.5 | loop fusion | flops 7077888 | bytes 14155776 | tf_op jit(solution)/shard_map/concatenate | solution.py:17
  105.8 11.3 %gather_fusion = bf16[81,192,512]{2,1,0:T(8,128)(2,1)} fusion(bf16[36,192,512]{2,1,0:T(8,128)(2,1)} %pad_maximum_fusion, s32[1024]{0:T(1024)S(1)} %pad_clamp_fusion), kind=kCustom, calls=%fused_computation | custom fusion | bytes 31850820 | tf_op jit(solution)/shard_map/jit(_take)/gather | solution.py:24
  117.1 10.4 %fusion.4 = f32[3,192,512]{2,1,0:T(8,128)S(1)} fusion(bf16[3,27,192,192]{3,2,1,0:T(8,128)(2,1)} %reshape.51, bf16[3,27,192,512]{3,2,1,0:T(8,128)(2,1)} %bitcast.22, pred[3,27]{1,0:T(4,128)(4,1)S(1)} %get-tuple-element.7), kind=kOutput, calls=%fused_computation.6 | convolution fusion | flops 3065610240 | bytes 23076944 | tf_op jit(solution)/shard_map/bkrc,bkcp->brp/dot_general | solution.py:26
  127.5 0.1 slice_bitcast_fusion.3
  127.7 0.1 pad_maximum_fusion.1
  127.7 0.0 copy-start.1
  127.8 0.0 copy-start.2
  127.8 0.0 copy-start.3
  127.8 20.3 %all_to_all.5 = f32[4,3,192,128]{3,2,1,0:T(8,128)S(1)} all-to-all(f32[4,3,192,128]{3,2,1,0:T(8,128)S(1)} %pad_maximum_fusion.1), channel_id=1, replica_groups=mesh['slab'=64,'grp'=4] {'grp'}, dimensions={0} | all-to-all | bytes 2359296 | tf_op jit(solution)/shard_map/all_to_all | solution.py:41
  148.1 0.1 broadcast_multiply_fusion
  148.2 0.0 copy-done.1
  148.2 0.0 copy-done.2
  148.2 0.0 copy-done.3
  148.2 1.3 multiply_reduce_fusion.1
  149.5 158.0 %all-reduce = (f32[1,128]{1,0:T(1,128)S(1)}, f32[1,128]{1,0:T(1,128)S(1)}) all-reduce(f32[1,128]{1,0:T(1,128)S(1)} %bitcast.24, f32[1,128]{1,0:T(1,128)S(1)} %bitcast.23), channel_id=1, replica_groups=mesh['slab'=64,'grp'=4] {'slab'}, use_global_device_ids=true, to_apply=%region_3.4 | all-reduce | flops 256 | bytes 2048 | tf_op jit(solution)/shard_map/psum | solution.py:47
  307.5 0.6 maximum_multiply_fusion
  (3 shorter events, 0.0 us)
Async XLA Ops:
  7.2 34.8 %all-gather.2.cloned.1.call-start = ((), (), s32[]{:S(2)}) async-start(), calls=%async_computation.1 | async-start | bytes 2949120 | tf_op jit(solution)/shard_map/all_gather | solution.py:37
  42.0 57.9 %collective-permute-start = (bf16[12,192,512]{2,1,0:T(8,128)(2,1)}, bf16[12,192,512]{2,1,0:T(8,128)(2,1)}, u32[]{:S(2)}, u32[]{:S(2)}) collective-permute-start(bf16[12,192,512]{2,1,0:T(8,128)(2,1)} %all-gather.2.cloned.1.call-done), channel_id=1, source_target_pairs={{0,4},{4,8},{8,12},{12,16},{16,20},{20,24},{24,28},{28,32},{32,36}... | collective-permute-start | bytes 7077896 | tf_op jit(solution)/shard_map/ppermute | solution.py:15
  43.6 56.4 %collective-permute-start.1 = (bf16[12,192,512]{2,1,0:T(8,128)(2,1)}, bf16[12,192,512]{2,1,0:T(8,128)(2,1)}, u32[]{:S(2)}, u32[]{:S(2)}) collective-permute-start(bf16[12,192,512]{2,1,0:T(8,128)(2,1)} %all-gather.2.cloned.1.call-done), channel_id=1, source_target_pairs={{4,0},{8,4},{12,8},{16,12},{20,16},{24,20},{28,24},{32,28},{36,32}... | collective-permute-start | bytes 7077896 | tf_op jit(solution)/shard_map/ppermute | solution.py:16
  49.8 50.2 %copy-start = (bf16[12,192,512]{2,1,0:T(8,128)(2,1)S(1)}, bf16[12,192,512]{2,1,0:T(8,128)(2,1)}, u32[]{:S(2)}) copy-start(bf16[12,192,512]{2,1,0:T(8,128)(2,1)} %all-gather.2.cloned.1.call-done) | copy-start | bytes 7077892
  127.7 20.4 %copy-start.1 = (bf16[12,192,128]{2,1,0:T(8,128)(2,1)S(1)}, bf16[12,192,128]{2,1,0:T(8,128)(2,1)}, u32[]{:S(2)}) copy-start(bf16[12,192,128]{2,1,0:T(8,128)(2,1)} %param.7) | copy-start | bytes 1769476
  127.8 20.4 %copy-start.2 = (f32[12,192,128]{2,1,0:T(8,128)S(1)}, f32[12,192,128]{2,1,0:T(8,128)}, u32[]{:S(2)}) copy-start(f32[12,192,128]{2,1,0:T(8,128)} %param.9) | copy-start | bytes 3538948
  127.8 20.4 %copy-start.3 = (f32[12,192,128]{2,1,0:T(8,128)S(1)}, f32[12,192,128]{2,1,0:T(8,128)}, u32[]{:S(2)}) copy-start(f32[12,192,128]{2,1,0:T(8,128)} %param.8) | copy-start | bytes 3538948
Sparse Core Ops, SparseCore 0:
  9.8 32.1 all-gather.1
